TPU v7x, 256 devices: a whole 4x4x8 slice. The times are simulated.
256 devices in a mesh: tm: 8 (over z_hi, y), aux: 32 (over z_lo, x, core).
Axes of the slice: x: 4, y: 4, z: 8 (z_hi: 2, z_lo: 4; z = z_hi * 4 + z_lo), core: 2. Of those that a mesh axis runs over, the one named last changes fastest.
Arguments:
- green: bfloat16 [16, 1024, 1024], P('tm'), may hold values from -4 to 4
- factors: bfloat16 [4096, 1024], P('aux'), may hold values from -0.1875 to 0.1875
- pattern: int32 [32, 8], P('aux'), may hold values 0 or 1
- coulomb: float32 [4096], P('aux'), may hold values from 0.5 to 2
Outputs:
- sigma: float32 [1024, 16, 1024], P('aux', 'tm')
All inputs are finite; a program needn't handle non-finite values. No bound on the sum of `pattern` on one device may be relied on, other than what follows from the above.
Results may differ from a plain program's by a relative error of at most 0.006.
Values may be sent and summed in bfloat16 or wider, within the bound.
No kernel may reach another device: no remote copies, remote signals or barrier semaphores. Data moves between devices by JAX's collectives and lax.ppermute only.
A program may use at most 64 MiB of HBM per device.

v0:
```python
import jax
import jax.numpy as jnp
from jax import lax
from jax.sharding import PartitionSpec as P

BLOCK = 128


def local(green, factors, pattern, coulomb):
    f32, bf16 = (jnp.float32, jnp.bfloat16)
    devices = lax.axis_size("aux")
    own = factors.shape[0]
    mask = jnp.repeat(jnp.repeat(pattern, BLOCK, axis=0), BLOCK, axis=1)
    masked = factors * mask.astype(factors.dtype)
    rows = lax.all_gather(masked, "aux", axis=0, tiled=True)
    left = jnp.einsum("qo,tok->tqk", masked, green, preferred_element_type=f32).astype(bf16)
    half = lax.axis_size("tm") // 2
    left = lax.ppermute(left, "tm", [(i, (i + half) % (2 * half)) for i in range(2 * half)])
    right = jnp.einsum("qo,tko->tqk", masked, green, preferred_element_type=f32).astype(bf16)
    weights = lax.all_gather(coulomb, "aux", axis=0, tiled=True)
    aux_green = jnp.einsum("tqo,po->tqp", right, rows, preferred_element_type=f32)
    mirror = jnp.einsum("tqo,po->tqp", left, rows, preferred_element_type=f32)
    kernel = aux_green * weights[None, None, :] * (aux_green * mirror) * coulomb[None, :, None]
    kernel = kernel.astype(bf16)
    part = jnp.einsum("tqp,pi->tqi", kernel, rows, preferred_element_type=f32).astype(bf16)
    times, orb = (green.shape[0], green.shape[1])
    part = part.reshape(times, own, devices, orb // devices).transpose(2, 0, 1, 3)
    part = lax.all_to_all(part, "aux", split_axis=0, concat_axis=0, tiled=True)
    rows = rows.reshape(devices, own, orb)
    return jnp.einsum("dtqi,dqj->itj", part, rows, preferred_element_type=f32)


def solution(mesh):
    in_specs = (P("tm", None, None), P("aux", None), P("aux", None), P("aux"))
    out_specs = P("aux", "tm", None)
    return jax.shard_map(local, mesh=mesh, in_specs=in_specs, out_specs=out_specs, check_vma=False)
```

profile of v0, /device:TPU:1, one launch (start us, length us, event | category | flops | bytes accessed | tf_op | source)
XLA Modules:
  0.0 154.6 jit_solution(5889969668802881452)
XLA Ops:
  6.5 0.0 copy-start.1
  6.5 0.0 all-gather.3.cloned.1.call-start
  6.5 0.7 convert_bitcast_fusion
  7.2 0.1 broadcast_bitcast_fusion
  7.3 1.7 %broadcast_multiply_fusion = bf16[128,1024]{1,0:T(8,128)(2,1)} fusion(bf16[128,1024]{1,0:T(8,128)(2,1)} %param.5, bf16[1024]{0:T(1024)(128)(2,1)S(1)} %broadcast_bitcast_fusion), kind=kLoop, calls=%fused_computation.20 | loop fusion | flops 131072 | bytes 526336 | tf_op jit(solution)/shard_map/mul | solution.py:14
  9.0 0.0 copy-start
  9.0 0.0 all-gather.3.cloned.1.call-update
  9.0 3.0 %fusion.28 = bf16[2,128,1024]{2,1,0:T(8,128)(2,1)S(1)} fusion(bf16[2,1024,1024]{2,1,0:T(8,128)(2,1)} %param.4, bf16[128,1024]{1,0:T(8,128)(2,1)} %broadcast_multiply_fusion), kind=kOutput, calls=%fused_computation.16 | convolution fusion | flops 537133056 | bytes 4980736 | tf_op jit(solution)/shard_map/qo,tok->tqk/dot_general | solution.py:16
  12.0 7.8 %collective-permute-start = (bf16[2,128,1024]{2,1,0:T(8,128)(2,1)S(1)}, bf16[2,128,1024]{2,1,0:T(8,128)(2,1)S(1)}, u32[]{:S(2)}, u32[]{:S(2)}) collective-permute-start(bf16[2,128,1024]{2,1,0:T(8,128)(2,1)S(1)} %fusion.28), channel_id=1, source_target_pairs={{0,128},{32,160},{64,192},{96,224},{128,0},{160,32},{192,64},{224,... | collective-permute-start | bytes 1572872 | tf_op jit(solution)/shard_map/ppermute | solution.py:18
  19.8 0.0 copy-done.1
  19.8 65.0 %all-gather = f32[32,1,128]{2,1,0:T(1,128)S(1)} all-gather(f32[1,1,128]{2,1,0:T(1,128)S(1)} %bitcast.62), channel_id=1, replica_groups=mesh['tm'=8,'aux'=32] {'aux'}, dimensions={0}, use_global_device_ids=true | all-gather | bytes 16896 | tf_op jit(solution)/shard_map/all_gather | solution.py:20
  84.8 12.6 %all-gather.3.cloned.1.call-done = bf16[4096,1024]{1,0:T(8,128)(2,1)} async-done(((bf16[128,1024]{1,0:T(8,128)(2,1)}), bf16[4096,1024]{1,0:T(8,128)(2,1)}) %all-gather.3.cloned.1.call-update) | async-done | bytes 8388624 | tf_op jit(solution)/shard_map/all_gather | solution.py:15
  97.4 0.0 copy-done
  97.4 10.4 %fusion.4 = f32[2,128,4096]{2,1,0:T(8,128)} fusion(bf16[4096,1024]{1,0:T(8,128)(2,1)} %all-gather.3.cloned.1.call-done, bf16[2,1024,1024]{2,1,0:T(8,128)(2,1)} %param.4, bf16[128,1024]{1,0:T(8,128)(2,1)S(1)} %copy-done), kind=kOutput, calls=%fused_computation.4 | convolution fusion | flops 2684616704 | bytes 17039360 | tf_op jit(solution)/shard_map/tqo,po->tqp/dot_general | solution.py:21
  107.8 0.0 collective-permute-done
  107.8 11.9 %fusion.22 = bf16[2,128,1024]{2,1,0:T(8,128)(2,1)S(1)} fusion(bf16[4096,1024]{1,0:T(8,128)(2,1)} %all-gather.3.cloned.1.call-done, f32[2,128,4096]{2,1,0:T(8,128)} %fusion.4, bf16[2,128,1024]{2,1,0:T(8,128)(2,1)S(1)} %collective-permute-done, f32[128]{0:T(128)S(1)} %copy-done.1, f32[4096]{0:T(1024)S(1)} %bitcast.61), kind=kOutput, calls=%fused_computation.12 | convolution fusion | flops 4300472320 | bytes 13648384 | tf_op jit(solution)/shard_map/tqp,pi->tqi/dot_general | solution.py:25
  119.6 0.3 copy.9
  119.9 0.1 copy.10
  120.0 21.9 %all_to_all.5 = bf16[32,2,128,32]{2,3,1,0:T(8,128)(2,1)S(1)} all-to-all(bf16[32,2,128,32]{2,3,1,0:T(8,128)(2,1)S(1)} %copy.10), channel_id=1, replica_groups=mesh['tm'=8,'aux'=32] {'aux'}, dimensions={0} | all-to-all | bytes 1048576 | tf_op jit(solution)/shard_map/all_to_all | solution.py:28
  141.9 5.0 %convolution_bitcast_fusion = f32[32,2,1024]{2,0,1:T(8,128)S(1)} fusion(bf16[32,128,1024,1]{2,1,3,0:T(8,128)(2,1)} %bitcast.63, bf16[32,2,128,32]{2,3,1,0:T(8,128)(2,1)S(1)} %all_to_all.5), kind=kOutput, calls=%fused_computation.17 | convolution fusion | flops 536870912 | bytes 9175040 | tf_op jit(solution)/shard_map/dtqi,dqj->itj/dot_general | solution.py:30
  146.9 0.9 copy.12
Async XLA Ops:
  6.5 13.3 %copy-start.1 = (f32[128]{0:T(128)S(1)}, f32[128]{0:T(128)}, u32[]{:S(2)}) copy-start(f32[128]{0:T(128)} %param.7) | copy-start | bytes 1540
  6.5 90.9 %all-gather.3.cloned.1.call-start = ((), (), s32[]{:S(2)}) async-start(), calls=%async_computation.1 | async-start | bytes 8650752 | tf_op jit(solution)/shard_map/all_gather | solution.py:15
  9.0 88.4 %copy-start = (bf16[128,1024]{1,0:T(8,128)(2,1)S(1)}, bf16[128,1024]{1,0:T(8,128)(2,1)}, u32[]{:S(2)}) copy-start(bf16[128,1024]{1,0:T(8,128)(2,1)} %broadcast_multiply_fusion) | copy-start | bytes 786436
  12.0 95.8 %collective-permute-start = (bf16[2,128,1024]{2,1,0:T(8,128)(2,1)S(1)}, bf16[2,128,1024]{2,1,0:T(8,128)(2,1)S(1)}, u32[]{:S(2)}, u32[]{:S(2)}) collective-permute-start(bf16[2,128,1024]{2,1,0:T(8,128)(2,1)S(1)} %fusion.28), channel_id=1, source_target_pairs={{0,128},{32,160},{64,192},{96,224},{128,0},{160,32},{192,64},{224,... | collective-permute-start | bytes 1572872 | tf_op jit(solution)/shard_map/ppermute | solution.py:18
Sparse Core Ops, SparseCore 0:
  9.2 88.1 all-gather.2
where the time goes:
time: 155 us
  blocking collectives  86.9 us (56%)
  matrix products  30.2 us (19%)
  between operations  13.4 us (9%)
  waiting for transfers between devices  12.6 us (8%)
  starting transfers between devices  7.83 us (5%)
  other arithmetic  2.34 us (2%)
    all_gather x1, blocking collectives, local(): weights = lax.all_gather(coulomb, 'aux', axis=0, tiled=True)  65 us
    all_to_all x1, blocking collectives, local(): part = lax.all_to_all(part, 'aux', split_axis=0, concat_axis=0, tiled=True)  21.9 us
    all_gather x1, waiting for transfers between devices, local(): rows = lax.all_gather(masked, 'aux', axis=0, tiled=True)  12.6 us
    dot_general x1, matrix products, local(): jnp.einsum('tqp,pi->tqi', kernel, rows, preferred_element_type=f32)  11.9 us
    dot_general x1, matrix products, local(): jnp.einsum('tqo,po->tqp', right, rows, preferred_element_type=f32)  10.4 us
    ppermute x1, starting transfers between devices, local(): lax.ppermute(left, 'tm', [(i, (i + half) % (2 * half)) for i in range(2 *...  7.83 us
    dot_general x1, matrix products, local(): return jnp.einsum('dtqi,dqj->itj', part, rows, preferred_element_type=f32)  4.96 us
  transfers between devices with their start and end apart: 2, of which 1 were waited for; matrix products, arithmetic and copies ran while one was open for 9% of the time, Pallas kernels for 0%

commit v1 on v0

--- a/solution.py
+++ b/solution.py
@@ -2,8 +2,16 @@
 import jax.numpy as jnp
 from jax import lax
 from jax.sharding import PartitionSpec as P
+from jax.lax import all_to_all, axis_size
 
 BLOCK = 128
+
+
+def _store_set(field_in, comm_axis):
+    z_new = axis_size(comm_axis)
+    extra = jnp.stack([field_in] * z_new, 0)
+    value_now = all_to_all(extra, comm_axis, 0, 0)
+    return jnp.concatenate(value_now, 0)
 
 
 def local(green, factors, pattern, coulomb):
@@ -12,7 +20,7 @@
     own = factors.shape[0]
     mask = jnp.repeat(jnp.repeat(pattern, BLOCK, axis=0), BLOCK, axis=1)
     masked = factors * mask.astype(factors.dtype)
-    rows = lax.all_gather(masked, "aux", axis=0, tiled=True)
+    rows = _store_set(masked, "aux")
     left = jnp.einsum("qo,tok->tqk", masked, green, preferred_element_type=f32).astype(bf16)
     half = lax.axis_size("tm") // 2
     left = lax.ppermute(left, "tm", [(i, (i + half) % (2 * half)) for i in range(2 * half)])

time: 155 us -> 299 us (1.93)
  blocking collectives: 86.9 us -> 239 us
  between operations: 13.4 us -> 0.06 us
  starting transfers between devices: 7.83 us -> 14.4 us
  waiting for transfers between devices: 12.6 us -> 8.29 us
  local copies, waits for them, and re-layouts: 1.32 us -> 5.61 us
    all_gather x1, blocking collectives: 65 us -> 192 us  [local(): weights = lax.all_gather(coulomb, 'aux', axis=0, tiled=True)]
    all_to_all x1, blocking collectives: 21.9 us -> 46.4 us  [local(): part = lax.all_to_all(part, 'aux', split_axis=0, concat_axis=0, tiled=True)]
    all_gather x1 -> x0, waiting for transfers between devices: 12.6 us -> none  [local(): rows = lax.all_gather(masked, 'aux', axis=0, tiled=True)]
    all_to_all x0 -> x1, starting transfers between devices: none -> 10.1 us  [_store_set(): value_now = all_to_all(extra, comm_axis, 0, 0)]
    all_to_all x0 -> x1, waiting for transfers between devices: none -> 8.29 us  [_store_set(): value_now = all_to_all(extra, comm_axis, 0, 0)]
    another operation x0 -> x1, local copies, waits for them, and re-layouts: none -> 4.3 us  [_store_set(): extra = jnp.stack([field_in] * z_new, 0)]
    ppermute x1, starting transfers between devices: 7.83 us -> 4.3 us  [local(): lax.ppermute(left, 'tm', [(i, (i + half) % (2 * half)) for i in range(2 *...]
  transfers between devices with their start and end apart: 2 -> 2, of which waited for: 1 -> 1; matrix products, arithmetic and copies ran while one was open for 9% -> 4% of each run, Pallas kernels for 0% -> 0%
where the time goes in v1:
time: 299 us
  blocking collectives  239 us (80%)
  matrix products  30.1 us (10%)
  starting transfers between devices  14.4 us (5%)
  waiting for transfers between devices  8.29 us (3%)
  local copies, waits for them, and re-layouts  5.61 us (2%)
    all_gather x1, blocking collectives, local(): weights = lax.all_gather(coulomb, 'aux', axis=0, tiled=True)  192 us
    all_to_all x1, blocking collectives, local(): part = lax.all_to_all(part, 'aux', split_axis=0, concat_axis=0, tiled=True)  46.4 us
    dot_general x1, matrix products, local(): jnp.einsum('tqp,pi->tqi', kernel, rows, preferred_element_type=f32)  11.9 us
    dot_general x1, matrix products, local(): jnp.einsum('tqo,po->tqp', right, rows, preferred_element_type=f32)  10.4 us
    all_to_all x1, starting transfers between devices, _store_set(): value_now = all_to_all(extra, comm_axis, 0, 0)  10.1 us
    all_to_all x1, waiting for transfers between devices, _store_set(): value_now = all_to_all(extra, comm_axis, 0, 0)  8.29 us
  transfers between devices with their start and end apart: 2, of which 1 were waited for; matrix products, arithmetic and copies ran while one was open for 4% of the time, Pallas kernels for 0%

profile of v1, /device:TPU:1, one launch (start us, length us, event | category | flops | bytes accessed | tf_op | source)
XLA Modules:
  0.0 298.7 jit_solution(8266163382021103572)
XLA Ops:
  0.0 0.7 convert_bitcast_fusion
  0.7 0.1 broadcast_bitcast_fusion
  0.7 1.0 broadcast_multiply_fusion
  1.7 4.3 %stack.2 = bf16[32,128,1024]{2,1,0:T(8,128)(2,1)} broadcast(bf16[128,1024]{1,0:T(8,128)(2,1)S(1)} %broadcast_multiply_fusion), dimensions={1,2} | broadcast | bytes 8650752 | tf_op jit(solution)/shard_map/stack | solution.py:12
  6.0 10.1 %all-to-all-start = ((bf16[32,128,1024]{2,1,0:T(8,128)(2,1)}), bf16[32,128,1024]{2,1,0:T(8,128)(2,1)}, u32[]{:S(2)}, u32[]{:S(2)}) async-start(bf16[32,128,1024]{2,1,0:T(8,128)(2,1)} %stack.2), calls=%async_computation | async-start | bytes 16777216 | tf_op jit(solution)/shard_map/all_to_all | solution.py:13
  16.1 0.0 copy-start
  16.1 2.9 fusion.6
  19.0 4.3 %collective-permute-start = (bf16[2,128,1024]{2,1,0:T(8,128)(2,1)S(1)}, bf16[2,128,1024]{2,1,0:T(8,128)(2,1)S(1)}, u32[]{:S(2)}, u32[]{:S(2)}) collective-permute-start(bf16[2,128,1024]{2,1,0:T(8,128)(2,1)S(1)} %fusion.6), channel_id=1, source_target_pairs={{0,128},{32,160},{64,192},{96,224},{128,0},{160,32},{192,64},{224,... | collective-permute-start | bytes 1572872 | tf_op jit(solution)/shard_map/ppermute | solution.py:26
  23.3 0.0 copy-done
  23.3 192.2 %all-gather = f32[32,1,128]{2,1,0:T(1,128)S(1)} all-gather(f32[1,1,128]{2,1,0:T(1,128)S(1)} %bitcast.48), channel_id=1, replica_groups=mesh['tm'=8,'aux'=32] {'aux'}, dimensions={0}, use_global_device_ids=true | all-gather | bytes 16896 | tf_op jit(solution)/shard_map/all_gather | solution.py:28
  215.5 8.3 %all-to-all-done = bf16[32,128,1024]{2,1,0:T(8,128)(2,1)} async-done(((bf16[32,128,1024]{2,1,0:T(8,128)(2,1)}), bf16[32,128,1024]{2,1,0:T(8,128)(2,1)}, u32[]{:S(2)}, u32[]{:S(2)}) %all-to-all-start) | async-done | bytes 8388640 | tf_op jit(solution)/shard_map/all_to_all | solution.py:13
  223.8 10.4 %fusion.10 = f32[2,128,4096]{2,1,0:T(8,128)} fusion(bf16[4096,1024,1]{1,0,2:T(8,128)(2,1)} %bitcast.5, bf16[2,1024,1024]{2,1,0:T(8,128)(2,1)} %param.4, bf16[128,1024]{1,0:T(8,128)(2,1)S(1)} %broadcast_multiply_fusion), kind=kOutput, calls=%fused_computation.12 | convolution fusion | flops 2684616704 | bytes 17039360 | tf_op jit(solution)/shard_map/tqo,po->tqp/dot_general | solution.py:29
  234.2 0.0 collective-permute-done
  234.2 11.9 %convolution_convert_fusion = bf16[2,128,1024]{2,1,0:T(8,128)(2,1)S(1)} fusion(bf16[4096,1024,1]{1,0,2:T(8,128)(2,1)} %bitcast.5, f32[2,128,4096]{2,1,0:T(8,128)} %fusion.10, bf16[2,128,1024]{2,1,0:T(8,128)(2,1)S(1)} %collective-permute-done, f32[128]{0:T(128)S(1)} %copy-done, f32[4096]{0:T(1024)S(1)} %bitcast.47), kind=kOutput, calls=%fused_computation.6 | convolution fusion | flops 4300472320 | bytes 13648384 | tf_op jit(solution)/shard_map/tqp,pi->tqi/dot_general | solution.py:33
  246.1 0.3 copy.9
  246.4 0.1 copy.10
  246.4 46.4 %all_to_all.10 = bf16[32,2,128,32]{2,3,1,0:T(8,128)(2,1)S(1)} all-to-all(bf16[32,2,128,32]{2,3,1,0:T(8,128)(2,1)S(1)} %copy.10), channel_id=1, replica_groups=mesh['tm'=8,'aux'=32] {'aux'}, dimensions={0} | all-to-all | bytes 1048576 | tf_op jit(solution)/shard_map/all_to_all | solution.py:36
  292.8 5.0 %fusion.7 = f32[32,2,1024]{2,0,1:T(8,128)S(1)} fusion(bf16[32,2,128,32]{2,3,1,0:T(8,128)(2,1)S(1)} %all_to_all.10, bf16[32,128,1024]{2,1,0:T(8,128)(2,1)} %all-to-all-done), kind=kOutput, calls=%fused_computation.11 | convolution fusion | flops 536870912 | bytes 9175040 | tf_op jit(solution)/shard_map/dtqi,dqj->itj/dot_general | solution.py:38
  297.8 0.9 copy.12
Async XLA Ops:
  6.0 217.8 %all-to-all-start = ((bf16[32,128,1024]{2,1,0:T(8,128)(2,1)}), bf16[32,128,1024]{2,1,0:T(8,128)(2,1)}, u32[]{:S(2)}, u32[]{:S(2)}) async-start(bf16[32,128,1024]{2,1,0:T(8,128)(2,1)} %stack.2), calls=%async_computation | async-start | bytes 16777216 | tf_op jit(solution)/shard_map/all_to_all | solution.py:13
  16.1 7.2 %copy-start = (f32[128]{0:T(128)S(1)}, f32[128]{0:T(128)}, u32[]{:S(2)}) copy-start(f32[128]{0:T(128)} %param.7) | copy-start | bytes 1540
  19.0 215.2 %collective-permute-start = (bf16[2,128,1024]{2,1,0:T(8,128)(2,1)S(1)}, bf16[2,128,1024]{2,1,0:T(8,128)(2,1)S(1)}, u32[]{:S(2)}, u32[]{:S(2)}) collective-permute-start(bf16[2,128,1024]{2,1,0:T(8,128)(2,1)S(1)} %fusion.6), channel_id=1, source_target_pairs={{0,128},{32,160},{64,192},{96,224},{128,0},{160,32},{192,64},{224,... | collective-permute-start | bytes 1572872 | tf_op jit(solution)/shard_map/ppermute | solution.py:26
